TPU v7x, 32 devices: a whole 2x2x4 slice. The times are simulated.
32 devices in a mesh: space: 16 (over z, x, core), tm: 2 (over y).
Axes of the slice: x: 2, y: 2, z: 4, core: 2. Of those that a mesh axis runs over, the one named last changes fastest.
Arguments:
- thermal_anomaly: bfloat16 [128, 140288], P('tm', 'space'), may hold values from -6 to 6
- smoothing_coefs: float32 [128], replicated, may hold values from -0.0075 to 0.0075
Outputs:
- orthonormal_basis: float32 [128, 140288], P(None, ('space', 'tm'))
- triangular_factor: float32 [128, 128], replicated
All inputs are finite; a program needn't handle non-finite values.
Results may differ from a plain program's by a relative error of at most 0.0003.
The roundings to bfloat16 on the way count: a program that leaves them out, or rounds other values in their place, can miss the bound.
Values may be sent and summed in bfloat16 or wider, within the bound.
A program may use at most 64 MiB of HBM per device.

v0:
```python
import jax
import jax.numpy as jnp
from jax import lax
from jax.sharding import PartitionSpec as P


def shifted(block, axis, distance):
    devices = range(lax.axis_size(axis))
    route = [(i - distance, i) for i in devices if i - distance in devices]
    return lax.ppermute(block, axis, route)


def banded_matrix(coefficients, count_rows, count_cols, delay_shift_amount):
    row_index = lax.broadcasted_iota(jnp.int32, (count_rows, count_cols), 0)
    col_index = lax.broadcasted_iota(jnp.int32, (count_rows, count_cols), 1)
    lag_index = row_index + delay_shift_amount - col_index
    length = coefficients.shape[0]
    inside = (lag_index >= 0) & (lag_index < length)
    safe = jnp.clip(lag_index, 0, length - 1)
    return jnp.where(inside, coefficients[safe], jnp.zeros((), coefficients.dtype))


def product_low(left, right):
    return jnp.dot(left, right.T, preferred_element_type=jnp.float32)


def summed_gram(panel):
    width_block = panel.shape[0] // 4
    pieces = [panel[index * width_block : (index + 1) * width_block] for index in range(4)]
    listing = []
    for row_block in range(4):
        for col_block in range(row_block + 1):
            listing.append(product_low(pieces[row_block], pieces[col_block]))
    stacked = lax.psum(jnp.stack(listing), ("space", "tm"))
    lookup = {}
    position = 0
    for row_block in range(4):
        for col_block in range(row_block + 1):
            lookup[row_block, col_block] = stacked[position]
            position = position + 1
    band_rows = []
    for row_block in range(4):
        entries = []
        for col_block in range(4):
            if col_block <= row_block:
                entries.append(lookup[row_block, col_block])
            else:
                entries.append(lookup[col_block, row_block].T)
        band_rows.append(jnp.concatenate(entries, axis=1))
    return jnp.concatenate(band_rows, axis=0)


def body(thermal_anomaly, smoothing_coefs):
    timesteps_each_shard = thermal_anomaly.shape[0]
    coefficients = jnp.concatenate([jnp.ones((1,), jnp.float32), smoothing_coefs]).astype(
        jnp.bfloat16
    )
    prior_timesteps = []
    for delay_shift_amount in (2, 1):
        prior_timesteps.append(shifted(thermal_anomaly, "tm", delay_shift_amount))
    extended_record = jnp.concatenate(prior_timesteps + [thermal_anomaly], axis=0)
    snapshot_array = banded_matrix(
        coefficients, timesteps_each_shard, 3 * timesteps_each_shard, 2 * timesteps_each_shard
    )
    outgoing = jnp.dot(snapshot_array, extended_record, preferred_element_type=jnp.float32).astype(
        jnp.bfloat16
    )
    arrived = lax.all_to_all(outgoing, "tm", split_axis=1, concat_axis=0, tiled=True)
    gram = summed_gram(arrived)
    lower_one = jnp.linalg.cholesky(gram)
    first_rows = jax.scipy.linalg.solve_triangular(
        lower_one, arrived.astype(jnp.float32), lower=True
    )
    location_total = thermal_anomaly.shape[1] * lax.axis_size("space")
    scale = jnp.sqrt(jnp.float32(location_total))
    return (first_rows * scale, lower_one / scale)


def solution(mesh):
    placed = (P("tm", "space"), P())
    return jax.shard_map(
        body, mesh=mesh, in_specs=placed, out_specs=(P(None, ("space", "tm")), P()), check_vma=False
    )
```

profile of v0, /device:TPU:0, one launch (start us, length us, event | category | flops | bytes accessed | tf_op | source)
XLA Modules:
  0.0 173.4 jit_solution(4869511577980264260)
XLA Ops:
  0.6 0.7 collective-permute-start
  1.4 5.9 %collective-permute-start.1 = (bf16[64,8768]{1,0:T(8,128)(2,1)}, bf16[64,8768]{1,0:T(8,128)(2,1)}, u32[]{:S(2)}, u32[]{:S(2)}) collective-permute-start(bf16[64,8768]{1,0:T(8,128)(2,1)} %param.2), channel_id=1, source_target_pairs={{0,1},{2,3},{4,5},{6,7},{8,9},{10,11},{12,13},{14,15},{16,17},{18,... | collective-permute-start | bytes 3366920 | tf_op jit(solution)/shard_map/ppermute | solution.py:10
  7.3 0.7 convert.4
  7.9 0.1 compare_select_fusion
  8.0 0.1 reshape.58
  8.1 0.1 pad_maximum_fusion.2
  8.2 0.0 copy-start
  8.2 72.2 %gather_fusion = bf16[12288]{0:T(1024)(128)(2,1)S(1)} fusion(bf16[129]{0:T(256)(128)(2,1)S(1)} %pad_maximum_fusion.2, s32[12288]{0:T(1024)S(1)} %broadcast_clamp_fusion), kind=kCustom, calls=%fused_computation | custom fusion | bytes 98304 | tf_op jit(solution)/shard_map/gather | solution.py:20
  80.4 0.1 reshape.57
  80.5 0.0 collective-permute-done
  80.5 0.0 collective-permute-done.1
  80.5 0.0 copy-done
  80.5 2.1 %convolution_convert_fusion = bf16[64,8768]{1,0:T(8,128)(2,1)S(1)} fusion(bf16[64,8768]{1,0:T(8,128)(2,1)S(1)} %copy-done, bf16[64,8768]{1,0:T(8,128)(2,1)} %collective-permute-done.1, bf16[64,8768]{1,0:T(8,128)(2,1)S(1)} %collective-permute-done, bf16[64,192]{1,0:T(8,128)(2,1)S(1)} %reshape.57, s32[64]{0:T(128)S(1)} %iota_add_fusion), kind=kOutput, calls=%fused_computation.1 | convolution fusion | flops 226205696 | bytes 4514048 | tf_op jit(solution)/shard_map/dot_general | solution.py:65
  82.6 1.2 all_to_all.14
  83.8 0.1 copy.76
  84.0 17.1 %all_to_all.19 = bf16[64,2,4384]{2,0,1:T(8,128)(2,1)S(1)} all-to-all(bf16[64,2,4384]{2,0,1:T(8,128)(2,1)S(1)} %copy.76), channel_id=1, replica_groups=mesh['space'=16,'tm'=2] {'tm'}, dimensions={1} | all-to-all | bytes 2244608 | tf_op jit(solution)/shard_map/all_to_all | solution.py:68
  101.1 0.2 fusion.14
  101.3 0.2 fusion.13
  101.5 0.2 fusion.12
  101.7 0.2 fusion.11
  101.9 0.2 fusion.10
  102.1 0.2 fusion.9
  102.4 0.2 fusion.8
  102.6 0.2 fusion.7
  102.8 0.2 fusion.6
  103.0 0.2 fusion.5
  103.3 42.9 %psum.7 = f32[10,32,32]{1,2,0:T(8,128)S(1)} all-reduce(f32[10,32,32]{1,2,0:T(8,128)S(1)} %fusion.5), channel_id=1, replica_groups=mesh['space'=16,'tm'=2] {'space','tm'}, use_global_device_ids=true, to_apply=%region_0.1 | all-reduce | flops 10240 | bytes 81920 | tf_op jit(solution)/shard_map/psum | solution.py:34
  146.2 0.1 copy.106
  146.2 0.1 copy.107
  146.3 0.1 copy.108
  146.4 0.1 copy.91
  146.4 0.1 copy.109
  146.5 0.1 pad_maximum_fusion
  146.6 0.1 copy.93
  146.7 0.1 copy.94
  146.8 0.1 maximum_maximum_fusion
  147.0 0.1 copy.95
  147.1 0.1 fusion.32
  147.2 11.7 %cholesky.16 = f32[128,128]{1,0:T(8,128)S(1)} custom-call(f32[128,128]{1,0:T(8,128)S(1)} %fusion.32), custom_call_target="Cholesky" | custom-call | tf_op jit(solution)/shard_map/jit(cholesky)/cholesky | solution.py:70
  158.9 0.6 compare_reduce_fusion
  159.6 1.3 fusion.37
  160.9 9.8 %custom-call.7 = f32[1,128,128]{1,2,0:T(8,128)S(1)} custom-call(f32[1,128,128]{2,1,0:T(8,128)S(1)} %get-tuple-element.18), custom_call_target="InvertDiagBlocksLowerTriangular" | custom-call | tf_op jit(solution)/shard_map/jit(_solve_triangular)/triangular_solve | solution.py:71
  170.7 2.7 %convolution_multiply_fusion = f32[128,4384]{0,1:T(8,128)} fusion(bf16[128,4384]{1,0:T(8,128)(2,1)S(1)} %bitcast.99, f32[1,128,128]{1,2,0:T(8,128)S(1)} %custom-call.7), kind=kOutput, calls=%fused_computation.2 | convolution fusion | flops 862490624 | bytes 3432448 | tf_op jit(solution)/shard_map/jit(_solve_triangular)/triangular_solve | solution.py:71
  (4 shorter events, 0.1 us)
Async XLA Ops:
  0.6 79.9 %collective-permute-start = (bf16[64,8768]{1,0:T(8,128)(2,1)}, bf16[64,8768]{1,0:T(8,128)(2,1)S(1)}, u32[]{:S(2)}, u32[]{:S(2)}) collective-permute-start(bf16[64,8768]{1,0:T(8,128)(2,1)} %param.2), channel_id=1, source_target_pairs={} | collective-permute-start | bytes 3366920 | tf_op jit(solution)/shard_map/ppermute | solution.py:10
  1.4 79.1 %collective-permute-start.1 = (bf16[64,8768]{1,0:T(8,128)(2,1)}, bf16[64,8768]{1,0:T(8,128)(2,1)}, u32[]{:S(2)}, u32[]{:S(2)}) collective-permute-start(bf16[64,8768]{1,0:T(8,128)(2,1)} %param.2), channel_id=1, source_target_pairs={{0,1},{2,3},{4,5},{6,7},{8,9},{10,11},{12,13},{14,15},{16,17},{18,... | collective-permute-start | bytes 3366920 | tf_op jit(solution)/shard_map/ppermute | solution.py:10
  8.2 72.3 %copy-start = (bf16[64,8768]{1,0:T(8,128)(2,1)S(1)}, bf16[64,8768]{1,0:T(8,128)(2,1)}, u32[]{:S(2)}) copy-start(bf16[64,8768]{1,0:T(8,128)(2,1)} %param.2) | copy-start | bytes 3366916
where the time goes:
time: 174 us; the launch traced here: 173 us
  local copies, waits for them, and re-layouts  74.4 us (43%)
  blocking collectives  60 us (34%)
  other arithmetic  24.7 us (14%)
  matrix products  6.89 us (4%)
  starting transfers between devices  6.63 us (4%)
    gather x2, local copies, waits for them, and re-layouts, banded_matrix(): coefficients[safe]  72.3 us
    psum x1, blocking collectives, summed_gram(): stacked = lax.psum(jnp.stack(listing), ('space', 'tm'))  42.9 us
    all_to_all x1, blocking collectives, body(): lax.all_to_all(outgoing, 'tm', split_axis=1, concat_axis=0, tiled=True)  17.1 us
    another operation x3, other arithmetic, body(): lower_one = jnp.linalg.cholesky(gram)  12.4 us
    another operation x1, other arithmetic, body(): jax.scipy.linalg.solve_triangular(lower_one, arrived.astype(jnp.float32),...  9.81 us
    ppermute x2, starting transfers between devices, shifted(): return lax.ppermute(block, axis, route)  6.63 us
  transfers between devices with their start and end apart: 2, of which 0 were waited for; matrix products, arithmetic and copies ran while one was open for 42% of the time, Pallas kernels for 0%

commit v1 on v0

--- a/solution.py
+++ b/solution.py
@@ -2,6 +2,7 @@
 import jax.numpy as jnp
 from jax import lax
 from jax.sharding import PartitionSpec as P
+from jax.lax import all_to_all, axis_size
 
 
 def shifted(block, axis, distance):
@@ -65,7 +66,10 @@
     outgoing = jnp.dot(snapshot_array, extended_record, preferred_element_type=jnp.float32).astype(
         jnp.bfloat16
     )
-    arrived = lax.all_to_all(outgoing, "tm", split_axis=1, concat_axis=0, tiled=True)
+    arrived = jnp.concatenate(
+        all_to_all(jnp.stack(jnp.split(outgoing, axis_size("tm"), axis=1), axis=0), "tm", 0, 0),
+        axis=0,
+    )
     gram = summed_gram(arrived)
     lower_one = jnp.linalg.cholesky(gram)
     first_rows = jax.scipy.linalg.solve_triangular(

time: 174 us -> 170 us (0.977)
  transfers between devices with their start and end apart: 2 -> 2, of which waited for: 0 -> 0; matrix products, arithmetic and copies ran while one was open for 42% -> 43% of each run, Pallas kernels for 0% -> 0%
where the time goes in v1:
time: 170 us
  local copies, waits for them, and re-layouts  73.3 us (43%)
  blocking collectives  59.9 us (35%)
  other arithmetic  24.8 us (15%)
  starting transfers between devices  5.7 us (3%)
  matrix products  5.63 us (3%)
    gather x2, local copies, waits for them, and re-layouts, banded_matrix(): coefficients[safe]  72.3 us
    psum x1, blocking collectives, summed_gram(): stacked = lax.psum(jnp.stack(listing), ('space', 'tm'))  42.9 us
    all_to_all x1, blocking collectives, body(): all_to_all(jnp.stack(jnp.split(outgoing, axis_size('tm'), axis=1), axis=0...  17.1 us
    another operation x3, other arithmetic, body(): lower_one = jnp.linalg.cholesky(gram)  12.4 us
    another operation x1, other arithmetic, body(): jax.scipy.linalg.solve_triangular(lower_one, arrived.astype(jnp.float32),...  9.81 us
    ppermute x2, starting transfers between devices, shifted(): return lax.ppermute(block, axis, route)  5.7 us
  transfers between devices with their start and end apart: 2, of which 0 were waited for; matrix products, arithmetic and copies ran while one was open for 43% of the time, Pallas kernels for 0%

profile of v1, /device:TPU:0, one launch (start us, length us, event | category | flops | bytes accessed | tf_op | source)
XLA Modules:
  0.0 170.2 jit_solution(11029027334082231849)
XLA Ops:
  0.6 0.7 collective-permute-start
  1.4 5.0 %collective-permute-start.1 = (bf16[64,8768]{1,0:T(8,128)(2,1)}, bf16[64,8768]{1,0:T(8,128)(2,1)S(1)}, u32[]{:S(2)}, u32[]{:S(2)}) collective-permute-start(bf16[64,8768]{1,0:T(8,128)(2,1)} %param.2), channel_id=1, source_target_pairs={{0,1},{2,3},{4,5},{6,7},{8,9},{10,11},{12,13},{14,15},{16,17},{18,... | collective-permute-start | bytes 3366920 | tf_op jit(solution)/shard_map/ppermute | solution.py:11
  6.3 0.7 convert.4
  7.0 0.1 compare_select_fusion
  7.1 0.1 reshape.59
  7.2 0.1 pad_maximum_fusion.3
  7.3 0.0 copy-start
  7.3 72.2 %gather_fusion = bf16[12288]{0:T(1024)(128)(2,1)S(1)} fusion(bf16[129]{0:T(256)(128)(2,1)S(1)} %pad_maximum_fusion.3, s32[12288]{0:T(1024)S(1)} %broadcast_clamp_fusion), kind=kCustom, calls=%fused_computation | custom fusion | bytes 98304 | tf_op jit(solution)/shard_map/gather | solution.py:21
  79.5 0.1 reshape.58
  79.6 0.0 collective-permute-done
  79.6 0.0 collective-permute-done.1
  79.6 0.0 copy-done
  79.6 0.8 convolution_convert_fusion
  80.4 0.2 slice_bitcast_fusion.1
  80.7 0.1 pad_maximum_fusion
  80.8 17.1 %all_to_all.5 = bf16[2,64,4384]{2,1,0:T(8,128)(2,1)S(1)} all-to-all(bf16[2,64,4384]{2,1,0:T(8,128)(2,1)S(1)} %pad_maximum_fusion), channel_id=1, replica_groups=mesh['space'=16,'tm'=2] {'tm'}, dimensions={0} | all-to-all | bytes 2244608 | tf_op jit(solution)/shard_map/all_to_all | solution.py:70
  97.9 0.2 fusion.14
  98.1 0.2 fusion.13
  98.3 0.2 fusion.12
  98.5 0.2 fusion.11
  98.7 0.2 fusion.10
  99.0 0.2 fusion.9
  99.2 0.2 fusion.8
  99.4 0.2 fusion.7
  99.6 0.2 fusion.6
  99.8 0.2 fusion.5
  100.1 42.9 %psum.7 = f32[10,32,32]{1,2,0:T(8,128)S(1)} all-reduce(f32[10,32,32]{1,2,0:T(8,128)S(1)} %fusion.5), channel_id=1, replica_groups=mesh['space'=16,'tm'=2] {'space','tm'}, use_global_device_ids=true, to_apply=%region_0.1 | all-reduce | flops 10240 | bytes 81920 | tf_op jit(solution)/shard_map/psum | solution.py:35
  143.0 0.1 copy.101
  143.0 0.1 copy.102
  143.1 0.1 copy.103
  143.2 0.1 copy.86
  143.2 0.1 copy.104
  143.3 0.1 pad_maximum_fusion.1
  143.4 0.1 copy.88
  143.5 0.1 copy.89
  143.6 0.1 maximum_maximum_fusion
  143.8 0.1 copy.90
  143.9 0.1 fusion.32
  144.0 11.7 %cholesky.16 = f32[128,128]{1,0:T(8,128)S(1)} custom-call(f32[128,128]{1,0:T(8,128)S(1)} %fusion.32), custom_call_target="Cholesky" | custom-call | tf_op jit(solution)/shard_map/jit(cholesky)/cholesky | solution.py:74
  155.7 0.6 compare_reduce_fusion
  156.4 1.3 fusion.37
  157.7 9.8 %custom-call.7 = f32[1,128,128]{1,2,0:T(8,128)S(1)} custom-call(f32[1,128,128]{2,1,0:T(8,128)S(1)} %get-tuple-element.20), custom_call_target="InvertDiagBlocksLowerTriangular" | custom-call | tf_op jit(solution)/shard_map/jit(_solve_triangular)/triangular_solve | solution.py:75
  167.5 2.7 %convolution_multiply_fusion = f32[128,4384]{0,1:T(8,128)} fusion(bf16[128,4384]{1,0:T(8,128)(2,1)S(1)} %bitcast.101, f32[1,128,128]{1,2,0:T(8,128)S(1)} %custom-call.7), kind=kOutput, calls=%fused_computation.2 | convolution fusion | flops 862490624 | bytes 3432448 | tf_op jit(solution)/shard_map/jit(_solve_triangular)/triangular_solve | solution.py:75
  (4 shorter events, 0.1 us)
Async XLA Ops:
  0.6 79.0 %collective-permute-start = (bf16[64,8768]{1,0:T(8,128)(2,1)}, bf16[64,8768]{1,0:T(8,128)(2,1)S(1)}, u32[]{:S(2)}, u32[]{:S(2)}) collective-permute-start(bf16[64,8768]{1,0:T(8,128)(2,1)} %param.2), channel_id=1, source_target_pairs={} | collective-permute-start | bytes 3366920 | tf_op jit(solution)/shard_map/ppermute | solution.py:11
  1.4 78.2 %collective-permute-start.1 = (bf16[64,8768]{1,0:T(8,128)(2,1)}, bf16[64,8768]{1,0:T(8,128)(2,1)S(1)}, u32[]{:S(2)}, u32[]{:S(2)}) collective-permute-start(bf16[64,8768]{1,0:T(8,128)(2,1)} %param.2), channel_id=1, source_target_pairs={{0,1},{2,3},{4,5},{6,7},{8,9},{10,11},{12,13},{14,15},{16,17},{18,... | collective-permute-start | bytes 3366920 | tf_op jit(solution)/shard_map/ppermute | solution.py:11
  7.3 72.3 %copy-start = (bf16[64,8768]{1,0:T(8,128)(2,1)S(1)}, bf16[64,8768]{1,0:T(8,128)(2,1)}, u32[]{:S(2)}) copy-start(bf16[64,8768]{1,0:T(8,128)(2,1)} %param.2) | copy-start | bytes 3366916
